TPU v7x, 32 devices: a whole 2x2x4 slice. The times are simulated.
32 devices in a mesh: row: 4 (over z), rhs: 8 (over y, x, core).
Axes of the slice: x: 2, y: 2, z: 4, core: 2. Of those that a mesh axis runs over, the one named last changes fastest.
Arguments:
- rhs_blocks: bfloat16 [8, 4, 512, 16384], P(None, 'row', None, 'rhs'), may hold values from -6 to 6
- panel: bfloat16 [8, 4, 512, 1536], P(None, 'row', 'rhs'), may hold values from -0.1875 to 0.1875
- inverse_diag: bfloat16 [3, 512, 512], replicated, may hold values from -0.25 to 0.25
Outputs:
- updated: bfloat16 [8, 4, 512, 16384], P(None, 'row', None, 'rhs')
All inputs are finite; a program needn't handle non-finite values.
Results may differ from a plain program's by a relative error of at most 0.0056.
Values may be sent and summed in bfloat16 or wider, within the bound.
No kernel may reach another device: no remote copies, remote signals or barrier semaphores. Data moves between devices by JAX's collectives and lax.ppermute only.
A program may use at most 128 MiB of HBM per device.

v0:
```python
import jax
import jax.numpy as jnp
from jax import lax
from jax.sharding import PartitionSpec as P


def per_device(rhs_blocks, panel, inverse_diag):
    work = rhs_blocks[:, 0].astype(jnp.float32)
    row_rank = lax.axis_index("row")
    row_count = lax.axis_size("row")
    cycles = work.shape[0]
    size_block = inverse_diag.shape[1]
    steps_total = inverse_diag.shape[0]
    globals_idx = jnp.arange(cycles, dtype=jnp.int32) * row_count + row_rank
    full_panel = lax.all_gather(panel, "rhs", axis=2, tiled=True)[:, 0]
    solved_list = []
    head_rhs = lax.all_gather(rhs_blocks[0], "row", axis=0, tiled=True)
    head_piece = panel[0, 0][None, :, : (steps_total - 1) * size_block]
    head_rows = lax.all_gather(head_piece, ("row", "rhs"), axis=0, tiled=True)
    head_rows = head_rows.reshape(row_count, size_block, (steps_total - 1) * size_block)
    head_work = [head_rhs[index].astype(jnp.float32) for index in range(steps_total)]
    for block_step in range(steps_total):
        answer = jnp.dot(
            inverse_diag[block_step],
            head_work[block_step].astype(jnp.bfloat16),
            preferred_element_type=jnp.float32,
        ).astype(jnp.bfloat16)
        solved_list.append(answer)
        for index in range(block_step + 1, steps_total):
            coupling = head_rows[index, :, block_step * size_block : (block_step + 1) * size_block]
            head_work[index] = head_work[index] - jnp.dot(
                coupling, answer, preferred_element_type=jnp.float32
            )
    steps_idx = jnp.arange(steps_total, dtype=jnp.int32)
    column_mask = globals_idx[:, None] > steps_idx[None, :]
    column_mask = jnp.repeat(column_mask, size_block, axis=1)[:, None, :]
    masked = jnp.where(column_mask, full_panel, jnp.zeros_like(full_panel))
    stacked = jnp.concatenate(solved_list, axis=0)
    change = jnp.einsum("cij,jn->cin", masked, stacked, preferred_element_type=jnp.float32)
    work = work - change
    result = work.astype(jnp.bfloat16)
    for block_step in range(steps_total):
        result = jnp.where(
            (globals_idx == block_step)[:, None, None], solved_list[block_step][None], result
        )
    return result[:, None]


def solution(mesh):
    in_specs = (P(None, "row", None, "rhs"), P(None, "row", "rhs", None), P())
    out_specs = P(None, "row", None, "rhs")
    return jax.shard_map(
        per_device, mesh=mesh, in_specs=in_specs, out_specs=out_specs, check_vma=False
    )
```

profile of v0, /device:TPU:0, one launch (start us, length us, event | category | flops | bytes accessed | tf_op | source)
XLA Modules:
  0.0 342.8 jit_solution(9639382394178538930)
XLA Ops:
  6.5 0.0 all-gather.8.cloned.1.call-start
  6.5 3.2 slice.36
  9.7 0.0 all-gather.8.cloned.1.call-update
  9.7 0.0 all-gather.10.cloned.1.call-start
  9.8 0.9 slice_bitcast_fusion.12
  10.7 0.7 slice.52
  11.4 0.0 all-gather.10.cloned.1.call-update
  11.4 0.0 all-gather.6.cloned.1.call-start
  11.4 0.7 all-gather.6.cloned.1.call-update
  12.2 150.0 %all-gather.8.cloned.1.call-done = bf16[4,1,512,2048]{3,2,1,0:T(8,128)(2,1)} async-done(((bf16[1,1,512,2048]{3,2,1,0:T(8,128)(2,1)}), bf16[4,1,512,2048]{3,2,1,0:T(8,128)(2,1)}) %all-gather.8.cloned.1.call-update) | async-done | bytes 8388624 | tf_op jit(solution)/shard_map/all_gather | solution.py:17
  162.2 3.0 convolution_convert_fusion.2
  165.2 59.8 %all-gather.10.cloned.1.call-done = bf16[2048,1024]{1,0:T(8,128)(2,1)} async-done(((bf16[64,1024]{1,0:T(8,128)(2,1)}), bf16[2048,1024]{1,0:T(8,128)(2,1)}) %all-gather.10.cloned.1.call-update) | async-done | bytes 4194320 | tf_op jit(solution)/shard_map/all_gather | solution.py:19
  225.0 4.3 %fusion.11 = f32[2048,512]{0,1:T(8,128)} fusion(bf16[512,2048]{1,0:T(8,128)(2,1)S(1)} %convolution_convert_fusion.2, bf16[4,512,1024]{2,1,0:T(8,128)(2,1)} %bitcast.76), kind=kOutput, calls=%fused_computation.26 | convolution fusion | flops 1073741824 | bytes 6815744 | tf_op jit(solution)/shard_map/dot_general | solution.py:31
  229.3 5.6 %convolution_convert_fusion.1 = bf16[2048,512]{0,1:T(8,128)(2,1)} fusion(bf16[512,2048]{1,0:T(8,128)(2,1)S(1)} %convolution_convert_fusion.2, bf16[4,1,512,2048]{3,2,1,0:T(8,128)(2,1)} %all-gather.8.cloned.1.call-done, bf16[4,512,1024]{2,1,0:T(8,128)(2,1)} %bitcast.77, bf16[3,512,512]{2,1,0:T(8,128)(2,1)} %param.5), kind=kOutput, calls=%fused_computation.17 | convolution fusion | flops 2151677952 | bytes 7340032 | tf_op jit(solution)/shard_map/dot_general | solution.py:23
  235.0 7.9 %fusion.10 = bf16[512,2048]{1,0:T(8,128)(2,1)} fusion(f32[2048,512]{0,1:T(8,128)} %fusion.11, bf16[2048,512]{0,1:T(8,128)(2,1)} %convolution_convert_fusion.1, bf16[4,1,512,2048]{3,2,1,0:T(8,128)(2,1)} %all-gather.8.cloned.1.call-done, bf16[4,512,1024]{2,1,0:T(8,128)(2,1)} %bitcast.78, bf16[3,512,512]{2,1,0:T(8,128)(2,1)} %param.5), kind=kOutput, calls=%fused_computation.19 | convolution fusion | flops 2152726528 | bytes 11534336 | tf_op jit(solution)/shard_map/dot_general | solution.py:23
  242.9 54.8 %all-gather.6.cloned.1.call-done = bf16[8,1,512,1536]{3,2,1,0:T(8,128)(2,1)} async-done(((bf16[8,1,64,1536]{3,2,1,0:T(8,128)(2,1)}), bf16[8,1,512,1536]{3,2,1,0:T(8,128)(2,1)}) %all-gather.6.cloned.1.call-update) | async-done | bytes 12582928 | tf_op jit(solution)/shard_map/all_gather | solution.py:15
  297.7 0.1 broadcast_in_dim.73
  297.8 38.5 %select_bitcast_fusion = bf16[8,1,512,2048]{3,2,1,0:T(8,128)(2,1)} fusion(pred[8]{0:T(512)(128)(4,1)S(1)} %get-tuple-element.5, pred[8]{0:T(512)(128)(4,1)S(1)} %get-tuple-element.6, pred[8]{0:T(512)(128)(4,1)S(1)} %broadcast_compare_fusion.2, bf16[8,1,512,2048]{3,2,1,0:T(8,128)(2,1)} %param.3, bf16[8,1,512,1536]{3,2,1,0:T(8,128)(2,1)} %all-gather.6.cloned.1.call-done, ...), kind=kOutput, calls=%fused_computation.2 | convolution fusion | flops 25845301248 | bytes 52441112 | tf_op jit(solution)/shard_map/cij,jn->cin/dot_general | solution.py:39
  (4 shorter events, 0.0 us)
Async XLA Ops:
  6.5 155.7 %all-gather.8.cloned.1.call-start = ((), (), s32[]{:S(2)}) async-start(), calls=%async_computation.1 | async-start | bytes 10485760 | tf_op jit(solution)/shard_map/all_gather | solution.py:17
  9.7 215.3 %all-gather.10.cloned.1.call-start = ((), (), s32[]{:S(2)}) async-start(), calls=%async_computation.2 | async-start | bytes 4325376 | tf_op jit(solution)/shard_map/all_gather | solution.py:19
  11.4 286.3 %all-gather.6.cloned.1.call-start = ((), (), s32[]{:S(2)}) async-start(), calls=%async_computation | async-start | bytes 14155776 | tf_op jit(solution)/shard_map/all_gather | solution.py:15
Sparse Core Ops, SparseCore 0:
  9.8 152.3 all-gather.7
  165.1 59.9 all-gather.9
  226.9 70.7 all-gather.5
where the time goes:
time: 343 us
  waiting for transfers between devices  265 us (77%)
  matrix products  59.4 us (17%)
  between operations  13.2 us (4%)
  local copies, waits for them, and re-layouts  4.84 us (1%)
    all_gather x1, waiting for transfers between devices, per_device(): head_rhs = lax.all_gather(rhs_blocks[0], 'row', axis=0, tiled=True)  150 us
    all_gather x1, waiting for transfers between devices, per_device(): head_rows = lax.all_gather(head_piece, ('row', 'rhs'), axis=0, tiled=True)  59.8 us
    all_gather x1, waiting for transfers between devices, per_device(): full_panel = lax.all_gather(panel, 'rhs', axis=2, tiled=True)[:, 0]  54.8 us
    dot_general x1, matrix products, per_device(): jnp.einsum('cij,jn->cin', masked, stacked, preferred_element_type=jnp.flo...  38.5 us
    dot_general x3, matrix products, per_device(): jnp.dot(inverse_diag[block_step], head_work[block_step].astype(jnp.bfloat...  16.6 us
  transfers between devices with their start and end apart: 3, of which 3 were waited for; matrix products, arithmetic and copies ran while one was open for 7% of the time, Pallas kernels for 0%

commit v1 on v0

--- a/solution.py
+++ b/solution.py
@@ -14,7 +14,12 @@
     globals_idx = jnp.arange(cycles, dtype=jnp.int32) * row_count + row_rank
     full_panel = lax.all_gather(panel, "rhs", axis=2, tiled=True)[:, 0]
     solved_list = []
-    head_rhs = lax.all_gather(rhs_blocks[0], "row", axis=0, tiled=True)
+    ring = [rhs_blocks[0]]
+    for hop in range(3):
+        ring.append(lax.ppermute(ring[-1], "row", [(dev, (dev + 1) % 4) for dev in range(4)]))
+    head_rhs = jnp.roll(
+        jnp.concatenate(ring[::-1], axis=0), (lax.axis_index("row") + 1) * ring[0].shape[0], axis=0
+    )
     head_piece = panel[0, 0][None, :, : (steps_total - 1) * size_block]
     head_rows = lax.all_gather(head_piece, ("row", "rhs"), axis=0, tiled=True)
     head_rows = head_rows.reshape(row_count, size_block, (steps_total - 1) * size_block)

time: 343 us -> 269 us (0.78)
  waiting for transfers between devices: 265 us -> 173 us
  local copies, waits for them, and re-layouts: 4.84 us -> 20.8 us
    ppermute x0 -> x3, waiting for transfers between devices: none -> 164 us  [per_device(): lax.ppermute(ring[-1], 'row', [(dev, (dev + 1) % 4) for dev in range(4)])]
    all_gather x1 -> x0, waiting for transfers between devices: 150 us -> none  [per_device(): head_rhs = lax.all_gather(rhs_blocks[0], 'row', axis=0, tiled=True)]
    all_gather x1, waiting for transfers between devices: 59.8 us -> 0.02 us  [per_device(): head_rows = lax.all_gather(head_piece, ('row', 'rhs'), axis=0, tiled=True)]
    all_gather x1, waiting for transfers between devices: 54.8 us -> 7.67 us  [per_device(): full_panel = lax.all_gather(panel, 'rhs', axis=2, tiled=True)[:, 0]]
    unnamed x0 -> x9, local copies, waits for them, and re-layouts: none -> 15.7 us
  transfers between devices with their start and end apart: 3 -> 5, of which waited for: 3 -> 4; matrix products, arithmetic and copies ran while one was open for 7% -> 12% of each run, Pallas kernels for 0% -> 0%
where the time goes in v1:
time: 269 us; the launch traced here: 268 us
  waiting for transfers between devices  173 us (64%)
  matrix products  58.2 us (22%)
  local copies, waits for them, and re-layouts  20.8 us (8%)
  between operations  13.5 us (5%)
  starting transfers between devices  3.15 us (1%)
    ppermute x3, waiting for transfers between devices, per_device(): lax.ppermute(ring[-1], 'row', [(dev, (dev + 1) % 4) for dev in range(4)])  164 us
    dot_general x1, matrix products, per_device(): jnp.einsum('cij,jn->cin', masked, stacked, preferred_element_type=jnp.flo...  38.5 us
    unnamed x9, local copies, waits for them, and re-layouts  15.7 us
    dot_general x3, matrix products, per_device(): jnp.dot(inverse_diag[block_step], head_work[block_step].astype(jnp.bfloat...  15.5 us
    all_gather x1, waiting for transfers between devices, per_device(): full_panel = lax.all_gather(panel, 'rhs', axis=2, tiled=True)[:, 0]  7.67 us
  transfers between devices with their start and end apart: 5, of which 4 were waited for; matrix products, arithmetic and copies ran while one was open for 12% of the time, Pallas kernels for 0%

profile of v1, /device:TPU:0, one launch (start us, length us, event | category | flops | bytes accessed | tf_op | source)
XLA Modules:
  0.0 268.3 jit_solution(17085174920798541810)
XLA Ops:
  6.5 0.0 all-gather.6.cloned.1.call-start
  6.5 0.9 slice_bitcast_fusion.9
  7.5 0.7 slice.48
  8.1 0.0 all-gather.6.cloned.1.call-update
  8.2 0.0 all-gather.4.cloned.1.call-start
  8.2 0.7 all-gather.4.cloned.1.call-update
  8.9 1.7 slice_bitcast_fusion
  10.6 3.1 %collective-permute-start = (bf16[1,512,2048]{2,1,0:T(8,128)(2,1)S(1)}, bf16[1,512,2048]{2,1,0:T(8,128)(2,1)S(1)}, u32[]{:S(2)}, u32[]{:S(2)}) collective-permute-start(bf16[1,512,2048]{2,1,0:T(8,128)(2,1)S(1)} %slice_bitcast_fusion), channel_id=1, source_target_pairs={{0,8},{8,16},{16,24},{24,0},{1,9},{9,17},{17,25},{25,1},{2,10},{10... | collective-permute-start | bytes 6291464 | tf_op jit(solution)/shard_map/ppermute | solution.py:19
  13.7 50.4 %collective-permute-done = bf16[1,512,2048]{2,1,0:T(8,128)(2,1)S(1)} collective-permute-done((bf16[1,512,2048]{2,1,0:T(8,128)(2,1)S(1)}, bf16[1,512,2048]{2,1,0:T(8,128)(2,1)S(1)}, u32[]{:S(2)}, u32[]{:S(2)}) %collective-permute-start) | collective-permute-done | bytes 2097184 | tf_op jit(solution)/shard_map/ppermute | solution.py:19
  64.2 0.0 collective-permute-start.1
  64.2 54.4 %collective-permute-done.1 = bf16[1,512,2048]{2,1,0:T(8,128)(2,1)} collective-permute-done((bf16[1,512,2048]{2,1,0:T(8,128)(2,1)S(1)}, bf16[1,512,2048]{2,1,0:T(8,128)(2,1)}, u32[]{:S(2)}, u32[]{:S(2)}) %collective-permute-start.1) | collective-permute-done | bytes 2097184 | tf_op jit(solution)/shard_map/ppermute | solution.py:19
  118.5 0.0 collective-permute-start.2
  118.6 59.4 %collective-permute-done.2 = bf16[1,512,2048]{2,1,0:T(8,128)(2,1)} collective-permute-done((bf16[1,512,2048]{2,1,0:T(8,128)(2,1)}, bf16[1,512,2048]{2,1,0:T(8,128)(2,1)}, u32[]{:S(2)}, u32[]{:S(2)}) %collective-permute-start.2) | collective-permute-done | bytes 2097184 | tf_op jit(solution)/shard_map/ppermute | solution.py:19
  178.0 1.7 constant_dynamic-update-slice_fusion.7
  179.7 1.7 constant_dynamic-update-slice_fusion.6
  181.4 0.1 constant_dynamic-update-slice_fusion.5
  181.6 1.7 constant_dynamic-update-slice_fusion.4
  183.3 1.7 constant_dynamic-update-slice_fusion.3
  185.1 2.4 constant_dynamic-update-slice_fusion.2
  187.4 0.1 constant_dynamic-update-slice_fusion.1
  187.6 1.7 constant_dynamic-update-slice_fusion
  189.3 0.0 copy-start
  189.3 6.2 %copy-done = bf16[8,512,2048]{2,1,0:T(8,128)(2,1)} copy-done((bf16[8,512,2048]{2,1,0:T(8,128)(2,1)}, bf16[8,512,2048]{2,1,0:T(8,128)(2,1)S(1)}, u32[]{:S(2)}) %copy-start) | copy-done | bytes 16777240
  195.5 2.3 convolution_convert_fusion.2
  197.8 0.0 all-gather.6.cloned.1.call-done
  197.8 4.2 %fusion.17 = f32[2048,512]{0,1:T(8,128)} fusion(bf16[2048,512]{0,1:T(8,128)(2,1)S(1)} %convolution_convert_fusion.2, bf16[4,512,1024]{2,1,0:T(8,128)(2,1)} %bitcast.79), kind=kOutput, calls=%fused_computation.29 | convolution fusion | flops 1073741824 | bytes 6815744 | tf_op jit(solution)/shard_map/dot_general | solution.py:36
  202.0 5.6 %convolution_convert_fusion.1 = bf16[2048,512]{0,1:T(8,128)(2,1)} fusion(bf16[8,512,2048]{2,1,0:T(8,128)(2,1)} %copy-done, s32[]{:T(128)S(6)} %add.39, bf16[2048,512]{0,1:T(8,128)(2,1)S(1)} %convolution_convert_fusion.2, bf16[4,512,1024]{2,1,0:T(8,128)(2,1)} %bitcast.80, bf16[3,512,512]{2,1,0:T(8,128)(2,1)} %param.5), kind=kOutput, calls=%fused_computation.17 | convolution fusion | flops 2151677952 | bytes 7340036 | tf_op jit(solution)/shard_map/dot_general | solution.py:28
  207.7 7.6 %fusion.10 = bf16[512,2048]{1,0:T(8,128)(2,1)} fusion(f32[2048,512]{0,1:T(8,128)} %fusion.17, bf16[8,512,2048]{2,1,0:T(8,128)(2,1)} %copy-done, s32[]{:T(128)S(6)} %add.38, bf16[2048,512]{0,1:T(8,128)(2,1)} %convolution_convert_fusion.1, bf16[4,512,1024]{2,1,0:T(8,128)(2,1)} %bitcast.81, bf16[3,512,512]{2,1,0:T(8,128)(2,1)} %param.5), kind=kOutput, calls=%fused_computation.19 | convolution fusion | flops 2152726528 | bytes 11534340 | tf_op jit(solution)/shard_map/dot_general | solution.py:28
  215.2 7.7 %all-gather.4.cloned.1.call-done = bf16[8,1,512,1536]{3,2,1,0:T(8,128)(2,1)} async-done(((bf16[8,1,64,1536]{3,2,1,0:T(8,128)(2,1)}), bf16[8,1,512,1536]{3,2,1,0:T(8,128)(2,1)}) %all-gather.4.cloned.1.call-update) | async-done | bytes 12582928 | tf_op jit(solution)/shard_map/all_gather | solution.py:15
  222.9 0.1 broadcast_in_dim.73
  223.0 38.5 %select_bitcast_fusion = bf16[8,1,512,2048]{3,2,1,0:T(8,128)(2,1)} fusion(pred[8]{0:T(512)(128)(4,1)S(1)} %get-tuple-element.5, pred[8]{0:T(512)(128)(4,1)S(1)} %get-tuple-element.6, pred[8]{0:T(512)(128)(4,1)S(1)} %broadcast_compare_fusion.2, bf16[8,1,512,2048]{3,2,1,0:T(8,128)(2,1)} %param.3, bf16[8,1,512,1536]{3,2,1,0:T(8,128)(2,1)} %all-gather.4.cloned.1.call-done, ...), kind=kOutput, calls=%fused_computation.2 | convolution fusion | flops 25845301248 | bytes 52441112 | tf_op jit(solution)/shard_map/cij,jn->cin/dot_general | solution.py:44
  (4 shorter events, 0.0 us)
Async XLA Ops:
  6.5 191.3 %all-gather.6.cloned.1.call-start = ((), (), s32[]{:S(2)}) async-start(), calls=%async_computation.1 | async-start | bytes 4325376 | tf_op jit(solution)/shard_map/all_gather | solution.py:24
  8.2 214.7 %all-gather.4.cloned.1.call-start = ((), (), s32[]{:S(2)}) async-start(), calls=%async_computation | async-start | bytes 14155776 | tf_op jit(solution)/shard_map/all_gather | solution.py:15
  10.6 53.5 %collective-permute-start = (bf16[1,512,2048]{2,1,0:T(8,128)(2,1)S(1)}, bf16[1,512,2048]{2,1,0:T(8,128)(2,1)S(1)}, u32[]{:S(2)}, u32[]{:S(2)}) collective-permute-start(bf16[1,512,2048]{2,1,0:T(8,128)(2,1)S(1)} %slice_bitcast_fusion), channel_id=1, source_target_pairs={{0,8},{8,16},{16,24},{24,0},{1,9},{9,17},{17,25},{25,1},{2,10},{10... | collective-permute-start | bytes 6291464 | tf_op jit(solution)/shard_map/ppermute | solution.py:19
  64.2 54.4 %collective-permute-start.1 = (bf16[1,512,2048]{2,1,0:T(8,128)(2,1)S(1)}, bf16[1,512,2048]{2,1,0:T(8,128)(2,1)}, u32[]{:S(2)}, u32[]{:S(2)}) collective-permute-start(bf16[1,512,2048]{2,1,0:T(8,128)(2,1)S(1)} %collective-permute-done), channel_id=1, source_target_pairs={{0,8},{8,16},{16,24},{24,0},{1,9},{9,17},{17,25},{25,1},{2,10},{10... | collective-permute-start | bytes 6291464 | tf_op jit(solution)/shard_map/ppermute | solution.py:19
  118.5 59.4 %collective-permute-start.2 = (bf16[1,512,2048]{2,1,0:T(8,128)(2,1)}, bf16[1,512,2048]{2,1,0:T(8,128)(2,1)}, u32[]{:S(2)}, u32[]{:S(2)}) collective-permute-start(bf16[1,512,2048]{2,1,0:T(8,128)(2,1)} %collective-permute-done.1), channel_id=1, source_target_pairs={{0,8},{8,16},{16,24},{24,0},{1,9},{9,17},{17,25},{25,1},{2,10},{10... | collective-permute-start | bytes 6291464 | tf_op jit(solution)/shard_map/ppermute | solution.py:19
  189.3 6.2 %copy-start = (bf16[8,512,2048]{2,1,0:T(8,128)(2,1)}, bf16[8,512,2048]{2,1,0:T(8,128)(2,1)S(1)}, u32[]{:S(2)}) copy-start(bf16[8,512,2048]{2,1,0:T(8,128)(2,1)S(1)} %constant_dynamic-update-slice_fusion) | copy-start | bytes 50331652
Sparse Core Ops, SparseCore 0:
  10.2 140.4 all-gather.5
  152.6 70.2 all-gather.3
